TPU v7x, 32 devices: a whole 2x2x4 slice. The times are simulated.
32 devices in a mesh: req: 8 (over z, y), tp: 4 (over x, core).
Axes of the slice: x: 2, y: 2, z: 4, core: 2. Of those that a mesh axis runs over, the one named last changes fastest.
Arguments:
- tokens: bfloat16 [16, 1024], P('req'), may hold values from -4 to 4
- slot_of: int32 [16], replicated, may hold values from 0 to 15, each once
- key_cache: bfloat16 [16, 1536, 1024], P('req', None, 'tp'), may hold values from -1100 to 1100
- value_cache: bfloat16 [16, 1536, 1024], P('req', None, 'tp'), may hold values from -6 to 6
- cache_len: int32 [16], P('req'), may hold values from 1 to 1536, as said below
- rel_bucket: int32 [16, 1536], P('req'), may hold values from 0 to 511
- rel_table: bfloat16 [512, 1024], P('req'), may hold values from -6 to 6
- w_query: bfloat16 [1024, 1024], P(None, 'tp'), may hold values from -0.1875 to 0.1875
- w_key: bfloat16 [1024, 1024], P(None, 'tp'), may hold values from -0.1875 to 0.1875
- w_out: bfloat16 [1024, 1024], P('tp'), may hold values from -0.1875 to 0.1875
- out_gain: float32 [1024], P('tp'), may hold values from 0.1 to 1.9
- out_bias: float32 [1024], P('tp'), may hold values from -0.5 to 0.5
Outputs:
- normed: bfloat16 [16, 1024], P('req', 'tp')
Inputs may be any that keep to these rules, and one draw needn't show every extreme that they name: slot_of names every slot exactly once. `cache_len`: some slot holds exactly 1536 live positions in every draw.
All inputs are finite; a program needn't handle non-finite values.
Results may differ from a plain program's by a relative error of at most 0.0034.
The roundings to bfloat16 on the way count: a program that leaves them out, or rounds other values in their place, can miss the bound.
Values may be sent and summed in bfloat16 or wider, within the bound.
No kernel may reach another device: no remote copies, remote signals or barrier semaphores. Data moves between devices by JAX's collectives and lax.ppermute only.
A program may use at most 64 MiB of HBM per device.

v0:
```python
import math
import jax
import jax.numpy as jnp
from jax import lax
from jax.sharding import PartitionSpec as P

HD = 64
BUCKETS = 512
MAXLEN = 1536
BLOCK = 512
epsilon = 1e-06
masked_score = -1e30


def norm_rows(matrix):
    row_mean = jnp.mean(matrix, axis=-1, keepdims=True)
    centred = matrix - row_mean
    variance = jnp.mean(centred * centred, axis=-1, keepdims=True)
    return centred * lax.rsqrt(variance + epsilon)


def project_rows(shard_rows, w_key, w_query):
    normed_rows = norm_rows(shard_rows.astype(jnp.float32)).astype(jnp.bfloat16)
    key_part = jnp.dot(normed_rows, w_key, preferred_element_type=jnp.float32).astype(jnp.bfloat16)
    query_part = jnp.dot(normed_rows, w_query, preferred_element_type=jnp.float32).astype(
        jnp.bfloat16
    )
    return jnp.concatenate((key_part, query_part), axis=1)


def block_scores(offset, key_rows, bucket_rows, query_heads, rel_key, rel_query):
    local_heads = query_heads.shape[0]
    block_keys = lax.dynamic_slice_in_dim(key_rows, offset, BLOCK, 0)
    forward = lax.dynamic_slice_in_dim(bucket_rows, offset, BLOCK, 0)
    backward = jnp.minimum(BUCKETS - forward, BUCKETS - 1)
    table_ids = jnp.arange(BUCKETS, dtype=jnp.int32)
    one_fwd = (forward[:, None] == table_ids[None, :]).astype(jnp.bfloat16)
    one_back = (backward[:, None] == table_ids[None, :]).astype(jnp.bfloat16)
    rows_fwd = jnp.dot(one_fwd, rel_key, preferred_element_type=jnp.float32).reshape(
        BLOCK, local_heads, HD
    )
    rows_back = jnp.dot(one_back, rel_query, preferred_element_type=jnp.float32).reshape(
        BLOCK, local_heads, HD
    )
    key_heads = block_keys.reshape(BLOCK, local_heads, HD)
    content = jnp.einsum("hd,jhd->hj", query_heads, key_heads, preferred_element_type=jnp.float32)
    along_key = jnp.einsum("hd,jhd->hj", query_heads.astype(jnp.float32), rows_fwd)
    against = jnp.sum(key_heads.astype(jnp.float32) * rows_back, axis=2).T
    return (content + along_key + against) * (1.0 / math.sqrt(3.0 * HD))


def attend_slot(query_own, key_rows, value_rows, bucket_rows, length, rel_key, rel_query):
    local_heads = query_own.shape[0] // HD
    query_heads = query_own.reshape(local_heads, HD)
    block_count = (length + BLOCK - 1) // BLOCK

    def block_step(block_index, buffer):
        offset = block_index * BLOCK
        block_part = block_scores(offset, key_rows, bucket_rows, query_heads, rel_key, rel_query)
        return lax.dynamic_update_slice_in_dim(buffer, block_part, offset, 1)

    scores = lax.fori_loop(
        0, block_count, block_step, jnp.full((local_heads, MAXLEN), masked_score, jnp.float32)
    )
    positions = jnp.arange(MAXLEN, dtype=jnp.int32)
    live_keys = (positions < length)[None, :]
    scores = jnp.where(live_keys, scores, masked_score)
    highest = jnp.max(scores, axis=1, keepdims=True)
    exponent = jnp.where(live_keys, jnp.exp(scores - highest), 0.0)
    weights = (exponent / jnp.sum(exponent, axis=1, keepdims=True)).astype(jnp.bfloat16)
    value_heads = value_rows.reshape(MAXLEN, local_heads, HD)
    context = jnp.einsum("hj,jhd->hd", weights, value_heads, preferred_element_type=jnp.float32)
    return context.reshape(local_heads * HD).astype(jnp.bfloat16)


def per_device(
    tokens,
    slot_of,
    key_cache,
    value_cache,
    cache_len,
    rel_bucket,
    rel_table,
    w_query,
    w_key,
    w_out,
    out_gain,
    out_bias,
):
    rows_dev = tokens.shape[0]
    col_width = w_query.shape[1]
    rel_both = project_rows(lax.all_gather(rel_table, "req", axis=0, tiled=True), w_key, w_query)
    rel_key = rel_both[:, :col_width]
    rel_query = rel_both[:, col_width:]
    queries = jnp.dot(tokens, w_query, preferred_element_type=jnp.float32).astype(jnp.bfloat16)
    all_queries = lax.all_gather(queries, "req", axis=0, tiled=True)
    first_row = lax.axis_index("req") * rows_dev
    own_rows = first_row + jnp.arange(rows_dev, dtype=jnp.int32)
    request_count = slot_of.shape[0]
    chooser = (slot_of[None, :] == own_rows[:, None]).astype(jnp.bfloat16)
    own_queries = jnp.dot(chooser, all_queries, preferred_element_type=jnp.float32).astype(
        jnp.bfloat16
    )
    contexts = []
    for slot_index in range(rows_dev):
        contexts.append(
            attend_slot(
                own_queries[slot_index],
                key_cache[slot_index],
                value_cache[slot_index],
                rel_bucket[slot_index],
                cache_len[slot_index],
                rel_key,
                rel_query,
            )
        )
    own_context = jnp.stack(contexts, axis=0)
    all_contexts = lax.all_gather(own_context, "req", axis=0, tiled=True)
    own_slots = lax.dynamic_slice_in_dim(slot_of, first_row, rows_dev, 0)
    picker = (own_slots[:, None] == jnp.arange(request_count, dtype=jnp.int32)[None, :]).astype(
        jnp.bfloat16
    )
    context_rows = jnp.dot(picker, all_contexts, preferred_element_type=jnp.float32).astype(
        jnp.bfloat16
    )
    partial_out = jnp.dot(context_rows, w_out, preferred_element_type=jnp.float32)
    col_start = lax.axis_index("tp") * col_width
    row_sum = lax.psum(partial_out, "tp")
    normed_full = norm_rows(row_sum + tokens.astype(jnp.float32))
    own_cols = lax.dynamic_slice_in_dim(normed_full, col_start, col_width, 1)
    return (own_cols * out_gain + out_bias).astype(jnp.bfloat16)


def solution(mesh):
    in_specs = (
        P("req", None),
        P(),
        P("req", None, "tp"),
        P("req", None, "tp"),
        P("req"),
        P("req", None),
        P("req", None),
        P(None, "tp"),
        P(None, "tp"),
        P("tp", None),
        P("tp"),
        P("tp"),
    )
    out_specs = P("req", "tp")
    return jax.shard_map(
        per_device, mesh=mesh, in_specs=in_specs, out_specs=out_specs, check_vma=False
    )
```

profile of v0, /device:TPU:0, one launch (start us, length us, event | category | flops | bytes accessed | tf_op | source)
XLA Modules:
  0.0 98.8 jit_solution(9995086282330034420)
XLA Ops:
  6.5 0.0 copy-start
  6.5 0.0 all-gather.4.cloned.1.call-start
  6.5 0.7 all-gather.4.cloned.1.call-update
  7.3 1.4 %fusion.53 = (s32[1]{0:T(128)}, s32[1]{0:T(128)}) fusion(s32[2]{0:T(128)} %param.20), kind=kLoop, calls=%fused_computation.89 | loop fusion | bytes 16 | tf_op jit(solution)/shard_map/slice | solution.py:112
  10.1 0.0 copy-done
  10.1 0.9 fusion.25
  10.9 22.3 %all-gather = bf16[8,2,256]{2,1,0:T(2,128)(2,1)S(1)} all-gather(bf16[1,2,256]{2,1,0:T(2,128)(2,1)S(1)} %fusion.25), channel_id=1, replica_groups=mesh['req'=8,'tp'=4] {'req'}, dimensions={0}, use_global_device_ids=true | all-gather | bytes 9216 | tf_op jit(solution)/shard_map/all_gather | solution.py:96
  33.2 0.7 dynamic_slice.18
  33.9 0.8 convolution_convert_fusion.4
  34.8 0.1 reshape_squeeze.12
  34.9 0.1 reshape_squeeze.14
  35.0 1.5 %fusion.51 = (bf16[1,1536,256]{2,1,0:T(8,128)(2,1)S(1)}, bf16[1,1536,256]{2,1,0:T(8,128)(2,1)S(1)}) fusion(bf16[2,1536,256]{2,1,0:T(8,128)(2,1)} %param.18), kind=kLoop, calls=%fused_computation.87 | loop fusion | bytes 3145728 | tf_op jit(solution)/shard_map/slice | solution.py:109
  36.5 1.2 %copy.33 = bf16[1,1536,256]{1,2,0:T(8,128)(2,1)} copy(bf16[1,1536,256]{2,1,0:T(8,128)(2,1)S(1)} %get-tuple-element.139) | data formatting | bytes 1572864
  37.6 1.2 %copy.35 = bf16[1,1536,256]{1,2,0:T(8,128)(2,1)} copy(bf16[1,1536,256]{2,1,0:T(8,128)(2,1)S(1)} %get-tuple-element.140) | data formatting | bytes 1572864
  38.8 1.5 %fusion.52 = (bf16[1,1536,256]{2,1,0:T(8,128)(2,1)S(1)}, bf16[1,1536,256]{2,1,0:T(8,128)(2,1)S(1)}) fusion(bf16[2,1536,256]{2,1,0:T(8,128)(2,1)} %param.19), kind=kLoop, calls=%fused_computation.88 | loop fusion | bytes 3145728 | tf_op jit(solution)/shard_map/slice | solution.py:110
  40.3 0.0 copy-start.4
  40.3 0.3 copy.34
  40.6 0.3 copy.36
  40.9 0.7 iota_compare_fusion.9
  41.6 0.7 iota_compare_fusion.8
  42.3 0.0 copy-done.4
  42.3 10.1 %all-gather.4.cloned.1.call-done = bf16[512,1024]{1,0:T(8,128)(2,1)} async-done(((bf16[64,1024]{1,0:T(8,128)(2,1)}), bf16[512,1024]{1,0:T(8,128)(2,1)}) %all-gather.4.cloned.1.call-update) | async-done | bytes 1048592 | tf_op jit(solution)/shard_map/all_gather | solution.py:92
  52.5 1.5 %convert_reduce_fusion = f32[512]{0:T(512)S(1)} fusion(bf16[512,1024]{1,0:T(8,128)(2,1)} %all-gather.4.cloned.1.call-done), kind=kLoop, calls=%fused_computation.35 | loop fusion | flops 1048064 | bytes 1050624 | tf_op jit(solution)/shard_map/reduce_sum | solution.py:16
  54.0 0.0 copy-done.1
  54.0 0.4 fusion.22
  54.4 0.5 convolution_convert_fusion
  54.9 0.5 copy-done.7
  55.5 0.5 convolution_convert_fusion.1
  56.0 2.4 %while.20 = (s32[]{:T(128)}, f32[4,1536]{1,0:T(4,128)S(1)}, s32[]{:T(128)}, bf16[1536,256]{0,1:T(8,128)(2,1)}, bf16[4,64]{1,0:T(4,128)(2,1)S(1)}, /*index=5*/s32...) while((s32[]{:T(128)}, f32[4,1536]{1,0:T(4,128)S(1)}, ...), condition=%wide.region_4.5_spmd, body=%wide.region_2.4_spmd.sunk | while | flops 269882368 | bytes 1903791 | solution.py:62
  56.0 0.1 subtract_minimum_fusion.4
  56.1 0.5 fusion.97
  56.6 0.1 fusion.98
  56.7 1.5 %multiply_reduce_fusion.5 = (f32[512,4]{0,1:T(4,128)S(1)}, bf16[512,256]{0,1:T(8,128)(2,1)S(1)}) fusion(bf16[1536,256]{0,1:T(8,128)(2,1)} %get-tuple-element.324, s32[]{:T(128)S(6)} %select_n.77, bf16[512,256]{1,0:T(8,128)(2,1)S(1)} %get-tuple-element.328, s32[512]{0:T(512)S(1)} %get-tuple-element.245), kind=kOutput, calls=%fused_computation.4.clone.1 | convolution fusion | flops 134871040 | bytes 796676 | tf_op jit(solution)/shard_map/while/body/dot_general | solution.py:42
  58.2 0.1 fusion.99
  58.4 0.1 select_reduce_fusion.1
  58.5 0.2 fusion.30
  58.7 0.1 fusion.32
  58.8 2.4 %while.21 = (s32[]{:T(128)}, f32[4,1536]{1,0:T(4,128)S(1)}, s32[]{:T(128)}, bf16[1536,256]{0,1:T(8,128)(2,1)}, bf16[4,64]{1,0:T(4,128)(2,1)S(1)}, /*index=5*/s32...) while((s32[]{:T(128)}, f32[4,1536]{1,0:T(4,128)S(1)}, ...), condition=%wide.region_9.10_spmd, body=%wide.region_7.9_spmd.sunk | while | flops 269882368 | bytes 1903791 | solution.py:62
  58.9 0.1 subtract_minimum_fusion.5
  58.9 0.5 fusion.107
  59.4 0.1 fusion.108
  59.6 1.5 %multiply_reduce_fusion.6 = (f32[512,4]{0,1:T(4,128)S(1)}, bf16[512,256]{0,1:T(8,128)(2,1)S(1)}) fusion(bf16[1536,256]{0,1:T(8,128)(2,1)} %get-tuple-element.288, s32[]{:T(128)S(6)} %select_n.78, bf16[512,256]{1,0:T(8,128)(2,1)S(1)} %get-tuple-element.292, s32[512]{0:T(512)S(1)} %get-tuple-element.257), kind=kOutput, calls=%fused_computation.21.clone.1 | convolution fusion | flops 134871040 | bytes 796676 | tf_op jit(solution)/shard_map/while/body/dot_general | solution.py:42
  61.1 0.1 fusion.109
  61.2 0.0 copy-start.2
  61.3 0.0 copy-start.3
  61.3 0.0 copy-start.5
  61.3 0.0 copy-start.6
  61.3 0.1 select_reduce_fusion
  61.4 0.2 fusion.31
  61.6 0.1 fusion.33
  61.7 0.3 fusion.28
  62.0 0.1 convert_element_type.81
  62.1 0.3 fusion.26
  62.4 0.1 convert_element_type.84
  62.6 22.3 %all-gather.1 = bf16[8,2,256]{2,1,0:T(2,128)(2,1)S(1)} all-gather(bf16[1,2,256]{2,1,0:T(2,128)(2,1)S(1)} %maximum_bitcast_fusion), channel_id=1, replica_groups=mesh['req'=8,'tp'=4] {'req'}, dimensions={0}, use_global_device_ids=true | all-gather | bytes 9216 | tf_op jit(solution)/shard_map/all_gather | solution.py:118
  84.9 0.0 copy-done.2
  84.9 0.3 fusion.24
  85.2 5.7 %psum.7 = f32[2,1024]{1,0:T(2,128)S(1)} all-reduce(f32[2,1024]{1,0:T(2,128)S(1)} %fusion.24), channel_id=1, replica_groups=mesh['req'=8,'tp'=4] {'tp'}, use_global_device_ids=true, to_apply=%region_12.13 | all-reduce | flops 2048 | bytes 16384 | tf_op jit(solution)/shard_map/psum | solution.py:128
  91.0 0.0 copy-done.3
  91.0 0.1 fusion.35
  91.1 0.2 multiply_reduce_fusion.2
  91.3 0.0 copy-done.5
  91.3 0.0 copy-done.6
  91.3 0.6 fusion.38
  (18 shorter events, 0.2 us)
Async XLA Ops:
  6.5 3.5 %copy-start = (bf16[1024,256]{1,0:T(8,128)(2,1)S(1)}, bf16[1024,256]{1,0:T(8,128)(2,1)}, u32[]{:S(2)}) copy-start(bf16[1024,256]{1,0:T(8,128)(2,1)} %param.23) | copy-start | bytes 1572868
  6.5 45.9 %all-gather.4.cloned.1.call-start = ((), (), s32[]{:S(2)}) async-start(), calls=%async_computation | async-start | bytes 1179648 | tf_op jit(solution)/shard_map/all_gather | solution.py:92
  40.3 2.0 %copy-start.4 = (s32[2,1536]{1,0:T(2,128)S(1)}, s32[2,1536]{1,0:T(2,128)}, u32[]{:S(2)}) copy-start(s32[2,1536]{1,0:T(2,128)} %param.21) | copy-start | bytes 36868
  52.5 1.5 %copy-start.1 = (bf16[512,1024]{1,0:T(8,128)(2,1)S(1)}, bf16[512,1024]{1,0:T(8,128)(2,1)}, u32[]{:S(2)}) copy-start(bf16[512,1024]{1,0:T(8,128)(2,1)} %all-gather.4.cloned.1.call-done) | copy-start | bytes 3145732
  54.4 1.0 %copy-start.7 = (bf16[1024,256]{1,0:T(8,128)(2,1)S(1)}, bf16[1024,256]{1,0:T(8,128)(2,1)}, u32[]{:S(2)}) copy-start(bf16[1024,256]{1,0:T(8,128)(2,1)} %param.24) | copy-start | bytes 1572868
  61.2 23.7 %copy-start.2 = (bf16[256,1024]{1,0:T(8,128)(2,1)S(1)}, bf16[256,1024]{1,0:T(8,128)(2,1)}, u32[]{:S(2)}) copy-start(bf16[256,1024]{1,0:T(8,128)(2,1)} %param.25) | copy-start | bytes 1572868
  61.3 29.7 %copy-start.3 = (bf16[2,1024]{1,0:T(2,128)(2,1)S(1)}, bf16[2,1024]{1,0:T(2,128)(2,1)}, u32[]{:S(2)}) copy-start(bf16[2,1024]{1,0:T(2,128)(2,1)} %param.16) | copy-start | bytes 12292
  61.3 30.1 %copy-start.5 = (f32[256]{0:T(256)S(1)}, f32[256]{0:T(256)}, u32[]{:S(2)}) copy-start(f32[256]{0:T(256)} %param.27) | copy-start | bytes 3076
  61.3 30.0 %copy-start.6 = (f32[256]{0:T(256)S(1)}, f32[256]{0:T(256)}, u32[]{:S(2)}) copy-start(f32[256]{0:T(256)} %param.26) | copy-start | bytes 3076
Sparse Core Ops, SparseCore 0:
  9.5 42.9 all-gather.3
where the time goes:
time: 99.3 us; the launch traced here: 98.8 us
  blocking collectives  50.3 us (51%)
  between operations  15 us (15%)
  waiting for transfers between devices  10.9 us (11%)
  local copies, waits for them, and re-layouts  8.97 us (9%)
  matrix products  8.17 us (8%)
  other arithmetic  5.37 us (5%)
    all_gather x1, blocking collectives, per_device(): all_contexts = lax.all_gather(own_context, 'req', axis=0, tiled=True)  22.3 us
    all_gather x1, blocking collectives, per_device(): all_queries = lax.all_gather(queries, 'req', axis=0, tiled=True)  22.3 us
    all_gather x1, waiting for transfers between devices, per_device(): lax.all_gather(rel_table, 'req', axis=0, tiled=True)  10.1 us
    psum x1, blocking collectives, per_device(): row_sum = lax.psum(partial_out, 'tp')  5.75 us
    unnamed x22, local copies, waits for them, and re-layouts  3.5 us
    dot_general x2, matrix products, block_scores(): jnp.dot(one_back, rel_query, preferred_element_type=jnp.float32)  2.97 us
  transfers between devices with their start and end apart: 1, of which 1 were waited for; matrix products, arithmetic and copies ran while one was open for 11% of the time, Pallas kernels for 0%

commit v1 on v0

--- a/solution.py
+++ b/solution.py
@@ -10,6 +10,15 @@
 BLOCK = 512
 epsilon = 1e-06
 masked_score = -1e30
+
+
+def sum_by_hops(x, mesh_axis):
+    n_dev = lax.axis_size(mesh_axis)
+    total, far = (x, 1)
+    while far < n_dev:
+        total = total + lax.ppermute(total, mesh_axis, [(i, i ^ far) for i in range(n_dev)])
+        far = 2 * far
+    return total
 
 
 def norm_rows(matrix):
@@ -125,7 +134,7 @@
     )
     partial_out = jnp.dot(context_rows, w_out, preferred_element_type=jnp.float32)
     col_start = lax.axis_index("tp") * col_width
-    row_sum = lax.psum(partial_out, "tp")
+    row_sum = sum_by_hops(partial_out, "tp")
     normed_full = norm_rows(row_sum + tokens.astype(jnp.float32))
     own_cols = lax.dynamic_slice_in_dim(normed_full, col_start, col_width, 1)
     return (own_cols * out_gain + out_bias).astype(jnp.bfloat16)

time: 99.3 us -> 98.4 us (level)
  blocking collectives: 50.3 us -> 44.6 us
  waiting for transfers between devices: 10.9 us -> 14.2 us
  starting transfers between devices: 0.01 us -> 1.46 us
    psum x1 -> x0, blocking collectives: 5.75 us -> none  [per_device(): row_sum = lax.psum(partial_out, 'tp')]
    ppermute x0 -> x2, waiting for transfers between devices: none -> 3.38 us  [sum_by_hops(): lax.ppermute(total, mesh_axis, [(i, i ^ far) for i in range(n_dev)])]
    ppermute x0 -> x2, starting transfers between devices: none -> 1.46 us  [sum_by_hops(): lax.ppermute(total, mesh_axis, [(i, i ^ far) for i in range(n_dev)])]
  transfers between devices with their start and end apart: 1 -> 3, of which waited for: 1 -> 3; matrix products, arithmetic and copies ran while one was open for 11% -> 12% of each run, Pallas kernels for 0% -> 0%
where the time goes in v1:
time: 98.4 us; the launch traced here: 97.9 us
  blocking collectives  44.6 us (45%)
  between operations  15 us (15%)
  waiting for transfers between devices  14.2 us (14%)
  local copies, waits for them, and re-layouts  8.97 us (9%)
  matrix products  8.17 us (8%)
  other arithmetic  5.37 us (5%)
  starting transfers between devices  1.46 us (1%)
    all_gather x1, blocking collectives, per_device(): all_contexts = lax.all_gather(own_context, 'req', axis=0, tiled=True)  22.3 us
    all_gather x1, blocking collectives, per_device(): all_queries = lax.all_gather(queries, 'req', axis=0, tiled=True)  22.3 us
    all_gather x1, waiting for transfers between devices, per_device(): lax.all_gather(rel_table, 'req', axis=0, tiled=True)  10.1 us
    unnamed x22, local copies, waits for them, and re-layouts  3.5 us
    ppermute x2, waiting for transfers between devices, sum_by_hops(): lax.ppermute(total, mesh_axis, [(i, i ^ far) for i in range(n_dev)])  3.38 us
    dot_general x2, matrix products, block_scores(): jnp.dot(one_back, rel_query, preferred_element_type=jnp.float32)  2.97 us
  transfers between devices with their start and end apart: 3, of which 3 were waited for; matrix products, arithmetic and copies ran while one was open for 12% of the time, Pallas kernels for 0%

profile of v1, /device:TPU:0, one launch (start us, length us, event | category | flops | bytes accessed | tf_op | source)
XLA Modules:
  0.0 97.9 jit_solution(10320661012566398594)
XLA Ops:
  6.5 0.0 copy-start
  6.5 0.0 all-gather.4.cloned.1.call-start
  6.5 0.7 all-gather.4.cloned.1.call-update
  7.3 1.4 %fusion.51 = (s32[1]{0:T(128)}, s32[1]{0:T(128)}) fusion(s32[2]{0:T(128)} %param.20), kind=kLoop, calls=%fused_computation.89 | loop fusion | bytes 16 | tf_op jit(solution)/shard_map/slice | solution.py:121
  10.1 0.0 copy-done
  10.1 0.9 fusion.25
  10.9 22.3 %all-gather = bf16[8,2,256]{2,1,0:T(2,128)(2,1)S(1)} all-gather(bf16[1,2,256]{2,1,0:T(2,128)(2,1)S(1)} %fusion.25), channel_id=1, replica_groups=mesh['req'=8,'tp'=4] {'req'}, dimensions={0}, use_global_device_ids=true | all-gather | bytes 9216 | tf_op jit(solution)/shard_map/all_gather | solution.py:105
  33.2 0.7 dynamic_slice.18
  33.9 0.8 convolution_convert_fusion.4
  34.8 0.1 reshape_squeeze.12
  34.9 0.1 reshape_squeeze.14
  35.0 1.5 %fusion.49 = (bf16[1,1536,256]{2,1,0:T(8,128)(2,1)S(1)}, bf16[1,1536,256]{2,1,0:T(8,128)(2,1)S(1)}) fusion(bf16[2,1536,256]{2,1,0:T(8,128)(2,1)} %param.18), kind=kLoop, calls=%fused_computation.87 | loop fusion | bytes 3145728 | tf_op jit(solution)/shard_map/slice | solution.py:118
  36.5 1.2 %copy.33 = bf16[1,1536,256]{1,2,0:T(8,128)(2,1)} copy(bf16[1,1536,256]{2,1,0:T(8,128)(2,1)S(1)} %get-tuple-element.139) | data formatting | bytes 1572864
  37.6 1.2 %copy.35 = bf16[1,1536,256]{1,2,0:T(8,128)(2,1)} copy(bf16[1,1536,256]{2,1,0:T(8,128)(2,1)S(1)} %get-tuple-element.140) | data formatting | bytes 1572864
  38.8 1.5 %fusion.50 = (bf16[1,1536,256]{2,1,0:T(8,128)(2,1)S(1)}, bf16[1,1536,256]{2,1,0:T(8,128)(2,1)S(1)}) fusion(bf16[2,1536,256]{2,1,0:T(8,128)(2,1)} %param.19), kind=kLoop, calls=%fused_computation.88 | loop fusion | bytes 3145728 | tf_op jit(solution)/shard_map/slice | solution.py:119
  40.3 0.0 copy-start.4
  40.3 0.3 copy.34
  40.6 0.3 copy.36
  40.9 0.7 iota_compare_fusion.9
  41.6 0.7 iota_compare_fusion.8
  42.3 0.0 copy-done.4
  42.3 10.1 %all-gather.4.cloned.1.call-done = bf16[512,1024]{1,0:T(8,128)(2,1)} async-done(((bf16[64,1024]{1,0:T(8,128)(2,1)}), bf16[512,1024]{1,0:T(8,128)(2,1)}) %all-gather.4.cloned.1.call-update) | async-done | bytes 1048592 | tf_op jit(solution)/shard_map/all_gather | solution.py:101
  52.5 1.5 %convert_reduce_fusion = f32[512]{0:T(512)S(1)} fusion(bf16[512,1024]{1,0:T(8,128)(2,1)} %all-gather.4.cloned.1.call-done), kind=kLoop, calls=%fused_computation.35 | loop fusion | flops 1048064 | bytes 1050624 | tf_op jit(solution)/shard_map/reduce_sum | solution.py:25
  54.0 0.0 copy-done.1
  54.0 0.4 fusion.22
  54.4 0.5 convolution_convert_fusion
  54.9 0.5 copy-done.7
  55.5 0.5 convolution_convert_fusion.1
  56.0 2.4 %while.20 = (s32[]{:T(128)}, f32[4,1536]{1,0:T(4,128)S(1)}, s32[]{:T(128)}, bf16[1536,256]{0,1:T(8,128)(2,1)}, bf16[4,64]{1,0:T(4,128)(2,1)S(1)}, /*index=5*/s32...) while((s32[]{:T(128)}, f32[4,1536]{1,0:T(4,128)S(1)}, ...), condition=%wide.region_4.5_spmd, body=%wide.region_2.4_spmd.sunk | while | flops 269882368 | bytes 1903791 | solution.py:71
  56.0 0.1 subtract_minimum_fusion.4
  56.1 0.5 fusion.95
  56.6 0.1 fusion.96
  56.7 1.5 %multiply_reduce_fusion.5 = (f32[512,4]{0,1:T(4,128)S(1)}, bf16[512,256]{0,1:T(8,128)(2,1)S(1)}) fusion(bf16[1536,256]{0,1:T(8,128)(2,1)} %get-tuple-element.324, s32[]{:T(128)S(6)} %select_n.77, bf16[512,256]{1,0:T(8,128)(2,1)S(1)} %get-tuple-element.328, s32[512]{0:T(512)S(1)} %get-tuple-element.245), kind=kOutput, calls=%fused_computation.4.clone.1 | convolution fusion | flops 134871040 | bytes 796676 | tf_op jit(solution)/shard_map/while/body/dot_general | solution.py:51
  58.2 0.1 fusion.97
  58.4 0.1 select_reduce_fusion.1
  58.5 0.2 fusion.30
  58.7 0.1 fusion.32
  58.8 2.4 %while.21 = (s32[]{:T(128)}, f32[4,1536]{1,0:T(4,128)S(1)}, s32[]{:T(128)}, bf16[1536,256]{0,1:T(8,128)(2,1)}, bf16[4,64]{1,0:T(4,128)(2,1)S(1)}, /*index=5*/s32...) while((s32[]{:T(128)}, f32[4,1536]{1,0:T(4,128)S(1)}, ...), condition=%wide.region_9.10_spmd, body=%wide.region_7.9_spmd.sunk | while | flops 269882368 | bytes 1903791 | solution.py:71
  58.9 0.1 subtract_minimum_fusion.5
  58.9 0.5 fusion.105
  59.4 0.1 fusion.106
  59.6 1.5 %multiply_reduce_fusion.6 = (f32[512,4]{0,1:T(4,128)S(1)}, bf16[512,256]{0,1:T(8,128)(2,1)S(1)}) fusion(bf16[1536,256]{0,1:T(8,128)(2,1)} %get-tuple-element.288, s32[]{:T(128)S(6)} %select_n.78, bf16[512,256]{1,0:T(8,128)(2,1)S(1)} %get-tuple-element.292, s32[512]{0:T(512)S(1)} %get-tuple-element.257), kind=kOutput, calls=%fused_computation.21.clone.1 | convolution fusion | flops 134871040 | bytes 796676 | tf_op jit(solution)/shard_map/while/body/dot_general | solution.py:51
  61.1 0.1 fusion.107
  61.2 0.0 copy-start.2
  61.3 0.0 copy-start.3
  61.3 0.0 copy-start.5
  61.3 0.0 copy-start.6
  61.3 0.1 select_reduce_fusion
  61.4 0.2 fusion.31
  61.6 0.1 fusion.33
  61.7 0.3 fusion.28
  62.0 0.1 convert_element_type.81
  62.1 0.3 fusion.26
  62.4 0.1 convert_element_type.84
  62.6 22.3 %all-gather.1 = bf16[8,2,256]{2,1,0:T(2,128)(2,1)S(1)} all-gather(bf16[1,2,256]{2,1,0:T(2,128)(2,1)S(1)} %maximum_bitcast_fusion), channel_id=1, replica_groups=mesh['req'=8,'tp'=4] {'req'}, dimensions={0}, use_global_device_ids=true | all-gather | bytes 9216 | tf_op jit(solution)/shard_map/all_gather | solution.py:127
  84.9 0.0 copy-done.2
  84.9 0.3 fusion.24
  85.2 0.0 collective-permute-start
  85.2 1.2 %collective-permute-done = f32[2,1024]{1,0:T(2,128)S(1)} collective-permute-done((f32[2,1024]{1,0:T(2,128)S(1)}, f32[2,1024]{1,0:T(2,128)S(1)}, u32[]{:S(2)}, u32[]{:S(2)}) %collective-permute-start) | collective-permute-done | bytes 8224 | tf_op jit(solution)/shard_map/ppermute | solution.py:19
  86.4 1.5 %collective-permute-start.1 = (f32[2,1024]{1,0:T(2,128)S(1)}, f32[2,1024]{1,0:T(2,128)S(1)}, u32[]{:S(2)}, u32[]{:S(2)}) collective-permute-start(f32[2,1024]{1,0:T(2,128)S(1)} %add.95), channel_id=1, source_target_pairs={{0,2},{1,3},{2,0},{3,1},{4,6},{5,7},{6,4},{7,5},{8,10},{9,11},{10,... | collective-permute-start | bytes 24584 | tf_op jit(solution)/shard_map/ppermute | solution.py:19
  87.9 2.2 %collective-permute-done.1 = f32[2,1024]{1,0:T(2,128)S(1)} collective-permute-done((f32[2,1024]{1,0:T(2,128)S(1)}, f32[2,1024]{1,0:T(2,128)S(1)}, u32[]{:S(2)}, u32[]{:S(2)}) %collective-permute-start.1) | collective-permute-done | bytes 8224 | tf_op jit(solution)/shard_map/ppermute | solution.py:19
  90.1 0.1 fusion.46
  90.2 0.2 multiply_reduce_fusion.2
  90.4 0.6 fusion.36
  (22 shorter events, 0.2 us)
Async XLA Ops:
  6.5 3.5 %copy-start = (bf16[1024,256]{1,0:T(8,128)(2,1)S(1)}, bf16[1024,256]{1,0:T(8,128)(2,1)}, u32[]{:S(2)}) copy-start(bf16[1024,256]{1,0:T(8,128)(2,1)} %param.23) | copy-start | bytes 1572868
  6.5 45.9 %all-gather.4.cloned.1.call-start = ((), (), s32[]{:S(2)}) async-start(), calls=%async_computation | async-start | bytes 1179648 | tf_op jit(solution)/shard_map/all_gather | solution.py:101
  40.3 2.0 %copy-start.4 = (s32[2,1536]{1,0:T(2,128)S(1)}, s32[2,1536]{1,0:T(2,128)}, u32[]{:S(2)}) copy-start(s32[2,1536]{1,0:T(2,128)} %param.21) | copy-start | bytes 36868
  52.5 1.5 %copy-start.1 = (bf16[512,1024]{1,0:T(8,128)(2,1)S(1)}, bf16[512,1024]{1,0:T(8,128)(2,1)}, u32[]{:S(2)}) copy-start(bf16[512,1024]{1,0:T(8,128)(2,1)} %all-gather.4.cloned.1.call-done) | copy-start | bytes 3145732
  54.4 1.0 %copy-start.7 = (bf16[1024,256]{1,0:T(8,128)(2,1)S(1)}, bf16[1024,256]{1,0:T(8,128)(2,1)}, u32[]{:S(2)}) copy-start(bf16[1024,256]{1,0:T(8,128)(2,1)} %param.24) | copy-start | bytes 1572868
  61.2 23.7 %copy-start.2 = (bf16[256,1024]{1,0:T(8,128)(2,1)S(1)}, bf16[256,1024]{1,0:T(8,128)(2,1)}, u32[]{:S(2)}) copy-start(bf16[256,1024]{1,0:T(8,128)(2,1)} %param.25) | copy-start | bytes 1572868
  61.3 28.8 %copy-start.3 = (bf16[2,1024]{1,0:T(2,128)(2,1)S(1)}, bf16[2,1024]{1,0:T(2,128)(2,1)}, u32[]{:S(2)}) copy-start(bf16[2,1024]{1,0:T(2,128)(2,1)} %param.16) | copy-start | bytes 12292
  61.3 29.1 %copy-start.5 = (f32[256]{0:T(256)S(1)}, f32[256]{0:T(256)}, u32[]{:S(2)}) copy-start(f32[256]{0:T(256)} %param.27) | copy-start | bytes 3076
  61.3 29.1 %copy-start.6 = (f32[256]{0:T(256)S(1)}, f32[256]{0:T(256)}, u32[]{:S(2)}) copy-start(f32[256]{0:T(256)} %param.26) | copy-start | bytes 3076
  85.2 1.2 %collective-permute-start = (f32[2,1024]{1,0:T(2,128)S(1)}, f32[2,1024]{1,0:T(2,128)S(1)}, u32[]{:S(2)}, u32[]{:S(2)}) collective-permute-start(f32[2,1024]{1,0:T(2,128)S(1)} %fusion.24), channel_id=1, source_target_pairs={{0,1},{1,0},{2,3},{3,2},{4,5},{5,4},{6,7},{7,6},{8,9},{9,8},{10,11... | collective-permute-start | bytes 24584 | tf_op jit(solution)/shard_map/ppermute | solution.py:19
  86.4 3.7 %collective-permute-start.1 = (f32[2,1024]{1,0:T(2,128)S(1)}, f32[2,1024]{1,0:T(2,128)S(1)}, u32[]{:S(2)}, u32[]{:S(2)}) collective-permute-start(f32[2,1024]{1,0:T(2,128)S(1)} %add.95), channel_id=1, source_target_pairs={{0,2},{1,3},{2,0},{3,1},{4,6},{5,7},{6,4},{7,5},{8,10},{9,11},{10,... | collective-permute-start | bytes 24584 | tf_op jit(solution)/shard_map/ppermute | solution.py:19
Sparse Core Ops, SparseCore 0:
  9.5 42.9 all-gather.3
